TPU v7x, 128 devices: a whole 4x4x4 slice. The times are simulated.
128 devices in a mesh: snap: 4 (over z_lo, core), pts: 32 (over z_hi, x, y).
Axes of the slice: x: 4, y: 4, z: 4 (z_hi: 2, z_lo: 2; z = z_hi * 2 + z_lo), core: 2. Of those that a mesh axis runs over, the one named last changes fastest.
Arguments:
- strains: bfloat16 [6, 512, 131072], P(None, 'snap', 'pts'), may hold values from -3 to 3
- moduli: float32 [2, 131072], P(None, 'pts'), may hold values from 0.5 to 2
- range_test: bfloat16 [131072, 256], P('pts'), may hold values from -0.015625 to 0.015625
- corange_test: bfloat16 [256, 512], replicated, may hold values from -0.25 to 0.25
- core_left: float32 [512, 512], P(None, 'snap'), may hold values from -0.25 to 0.25
- core_right: bfloat16 [512, 131072], P(None, 'pts'), may hold values from -0.015625 to 0.015625
Outputs:
- range_sketch: float32 [512, 256], P('snap')
- corange_sketch: float32 [256, 131072], P('snap', 'pts')
- core_sketch: float32 [512, 512], replicated
All inputs are finite; a program needn't handle non-finite values.
Results may differ from a plain program's by a relative error of at most 0.0031.
Values may be sent and summed in bfloat16 or wider, within the bound.
A program may use at most 64 MiB of HBM per device.

v0:
```python
import math
import jax
import jax.numpy as jnp
from jax import lax
from jax.sharding import PartitionSpec as P


def energy_field(strains, moduli):
    strain_xx = strains[0].astype(jnp.float32)
    strain_yy = strains[1].astype(jnp.float32)
    strain_zz = strains[2].astype(jnp.float32)
    strain_xy = strains[3].astype(jnp.float32)
    strain_yz = strains[4].astype(jnp.float32)
    strain_xz = strains[5].astype(jnp.float32)
    lame_first = moduli[0][None, :]
    shear_mod = moduli[1][None, :]
    strain_trace = strain_xx + strain_yy + strain_zz
    mean_strain = strain_trace / 3.0
    dev_xx = strain_xx - mean_strain
    dev_yy = strain_yy - mean_strain
    dev_zz = strain_zz - mean_strain
    dev_square = (
        dev_xx * dev_xx
        + dev_yy * dev_yy
        + dev_zz * dev_zz
        + 2.0 * (strain_xy * strain_xy + strain_yz * strain_yz + strain_xz * strain_xz)
    ) / 6.0
    dev_norm = jnp.sqrt(dev_square)
    dev_det = (
        dev_xx * (dev_yy * dev_zz - strain_yz * strain_yz)
        - strain_xy * (strain_xy * dev_zz - strain_yz * strain_xz)
        + strain_xz * (strain_xy * strain_yz - dev_yy * strain_xz)
    )
    sine_part = jnp.sqrt(
        jnp.maximum(4.0 * dev_square * dev_square * dev_square - dev_det * dev_det, 0.0)
    )
    angle_third = jnp.arctan2(sine_part, dev_det) / 3.0
    positive_trace = jnp.maximum(strain_trace, 0.0)
    density = 0.5 * lame_first * positive_trace * positive_trace
    for order in range(3):
        principal = mean_strain + 2.0 * dev_norm * jnp.cos(
            angle_third - 2.0 * math.pi * order / 3.0
        )
        positive = jnp.maximum(principal, 0.0)
        density = density + shear_mod * positive * positive
    return density.astype(jnp.bfloat16)


def per_device(strains, moduli, range_test, corange_test, core_left, core_right):
    energy = energy_field(strains, moduli)
    snap_rows = energy.shape[0]
    range_part = jnp.dot(energy, range_test, preferred_element_type=jnp.float32)
    cross_part = lax.dot_general(
        energy, core_right, (((1,), (1,)), ((), ())), preferred_element_type=jnp.float32
    )
    range_sketch = lax.psum(range_part, "pts")
    core_share = jnp.dot(core_left, cross_part, precision=lax.Precision.HIGHEST)
    core_sketch = lax.psum(core_share, ("snap", "pts"))
    own_cols = lax.dynamic_slice_in_dim(
        corange_test, lax.axis_index("snap") * snap_rows, snap_rows, 1
    )
    corange_sketch = lax.psum_scatter(
        jnp.dot(own_cols, energy, preferred_element_type=jnp.float32),
        "snap",
        scatter_dimension=0,
        tiled=True,
    )
    return (range_sketch, corange_sketch, core_sketch)


def solution(mesh):
    in_specs = (
        P(None, "snap", "pts"),
        P(None, "pts"),
        P("pts", None),
        P(),
        P(None, "snap"),
        P(None, "pts"),
    )
    out_specs = (P("snap", None), P("snap", "pts"), P())
    return jax.shard_map(
        per_device, mesh=mesh, in_specs=in_specs, out_specs=out_specs, check_vma=False
    )
```

profile of v0, /device:TPU:0, one launch (start us, length us, event | category | flops | bytes accessed | tf_op | source)
XLA Modules:
  0.0 557.0 jit_solution(8219614878723953401)
XLA Ops:
  8.0 0.0 copy-start
  8.0 0.0 all-reduce.5.cloned.1.call-start
  8.1 0.9 slice_multiply_fusion
  9.0 0.0 copy-start.1
  9.0 31.8 %fusion.11 = bf16[128,4096]{1,0:T(8,128)(2,1)S(1)} fusion(bf16[6,128,4096]{2,1,0:T(8,128)(2,1)} %param.6, f32[4096]{0:T(1024)S(1)} %bitcast.30, f32[4096]{0:T(1024)S(1)} %bitcast.29), kind=kLoop, calls=%fused_computation.30 | loop fusion | flops 36700160 | bytes 7372800 | tf_op jit(solution)/shard_map/convert_element_type | solution.py:46
  40.9 0.0 copy-done.1
  40.9 0.0 copy-start.2
  40.9 1.5 fusion.27
  42.4 0.0 copy-done.2
  42.4 2.0 convolution_bitcast_fusion
  44.4 0.0 all-reduce.5.cloned.1.call-update
  44.5 0.0 all-reduce.3.cloned.1.call-start
  44.5 0.0 copy-done
  44.5 1.1 fusion.26
  45.6 0.0 all-reduce.3.cloned.1.call-update
  45.7 0.0 reduce-scatter.2.cloned.1.call-start
  45.7 3.5 fusion.23
  49.2 0.0 reduce-scatter.2.cloned.1.call-update
  49.2 170.6 %all-reduce.5.cloned.1.call-done = f32[512,512]{0,1:T(8,128)} async-done(((f32[512,512]{0,1:T(8,128)}), f32[512,512]{0,1:T(8,128)}) %all-reduce.5.cloned.1.call-update) | async-done | bytes 1048592 | tf_op jit(solution)/shard_map/psum | solution.py:58
  219.8 2.5 copy.9
  222.3 325.7 %all-reduce.3.cloned.1.call-done = f32[128,256]{1,0:T(8,128)} async-done(((f32[128,256]{1,0:T(8,128)}), f32[128,256]{1,0:T(8,128)}) %all-reduce.3.cloned.1.call-update) | async-done | bytes 131088 | tf_op jit(solution)/shard_map/psum | solution.py:56
  548.0 0.0 reduce-scatter.2.cloned.1.call-done
  548.0 1.6 copy.12
Async XLA Ops:
  8.0 36.5 %copy-start = (bf16[4096,256]{1,0:T(8,128)(2,1)S(1)}, bf16[4096,256]{1,0:T(8,128)(2,1)}, u32[]{:S(2)}) copy-start(bf16[4096,256]{1,0:T(8,128)(2,1)} %param.8) | copy-start | bytes 6291460
  8.0 211.8 %all-reduce.5.cloned.1.call-start = ((), (), s32[]{:S(2)}) async-start(), calls=%async_computation.3 | async-start | bytes 2097152 | tf_op jit(solution)/shard_map/psum | solution.py:58
  9.0 31.9 %copy-start.1 = (bf16[512,4096]{1,0:T(8,128)(2,1)S(1)}, bf16[512,4096]{1,0:T(8,128)(2,1)}, u32[]{:S(2)}) copy-start(bf16[512,4096]{1,0:T(8,128)(2,1)} %param.11) | copy-start | bytes 12582916
  40.9 1.6 copy-start.2
  44.5 503.6 %all-reduce.3.cloned.1.call-start = ((), (), s32[]{:S(2)}) async-start(), calls=%async_computation.1 | async-start | bytes 262144 | tf_op jit(solution)/shard_map/psum | solution.py:56
  45.7 502.4 %reduce-scatter.2.cloned.1.call-start = ((), (), s32[]{:S(2)}) async-start(), calls=%async_computation.2 | async-start | bytes 5242880 | tf_op jit(solution)/shard_map/reduce_scatter | solution.py:62
Sparse Core Ops, SparseCore 0:
  44.6 175.1 all-reduce.4
  222.8 325.1 all-reduce.2
Sparse Core Ops, SparseCore 1:
  49.3 47.8 reduce-scatter.1
where the time goes:
time: 557 us
  waiting for transfers between devices  496 us (89%)
  other arithmetic  32.8 us (6%)
  between operations  15.6 us (3%)
  matrix products  8.11 us (1%)
    psum x1, waiting for transfers between devices, per_device(): range_sketch = lax.psum(range_part, 'pts')  326 us
    psum x1, waiting for transfers between devices, per_device(): core_sketch = lax.psum(core_share, ('snap', 'pts'))  171 us
    convert_element_type x1, other arithmetic, energy_field(): return density.astype(jnp.bfloat16)  31.8 us
  transfers between devices with their start and end apart: 3, of which 2 were waited for; matrix products, arithmetic and copies ran while one was open for 1% of the time, Pallas kernels for 0%

commit v1 on v0

--- a/solution.py
+++ b/solution.py
@@ -55,7 +55,8 @@
     )
     range_sketch = lax.psum(range_part, "pts")
     core_share = jnp.dot(core_left, cross_part, precision=lax.Precision.HIGHEST)
-    core_sketch = lax.psum(core_share, ("snap", "pts"))
+    inner = lax.psum(core_share, "snap")
+    core_sketch = lax.psum(inner, "pts")
     own_cols = lax.dynamic_slice_in_dim(
         corange_test, lax.axis_index("snap") * snap_rows, snap_rows, 1
     )

time: 557 us -> 497 us (0.89)
  waiting for transfers between devices: 496 us -> 438 us
    psum x1, waiting for transfers between devices: 171 us -> 42.7 us  [per_device(): inner = lax.psum(core_share, 'snap')]
    reduce_scatter x1, waiting for transfers between devices: 0.01 us -> 44.4 us  [per_device(): lax.psum_scatter(jnp.dot(own_cols, energy, preferred_element_type=jnp.flo...]
    psum x1, waiting for transfers between devices: 326 us -> 351 us  [per_device(): range_sketch = lax.psum(range_part, 'pts')]
  transfers between devices with their start and end apart: 3 -> 3, of which waited for: 2 -> 3; matrix products, arithmetic and copies ran while one was open for 1% -> 1% of each run, Pallas kernels for 0% -> 0%
where the time goes in v1:
time: 497 us; the launch traced here: 496 us
  waiting for transfers between devices  438 us (88%)
  other arithmetic  32.8 us (7%)
  between operations  13.8 us (3%)
  matrix products  8.11 us (2%)
    psum x1, waiting for transfers between devices, per_device(): range_sketch = lax.psum(range_part, 'pts')  351 us
    reduce_scatter x1, waiting for transfers between devices, per_device(): lax.psum_scatter(jnp.dot(own_cols, energy, preferred_element_type=jnp.flo...  44.4 us
    psum x1, waiting for transfers between devices, per_device(): inner = lax.psum(core_share, 'snap')  42.7 us
    convert_element_type x1, other arithmetic, energy_field(): return density.astype(jnp.bfloat16)  31.8 us
  transfers between devices with their start and end apart: 3, of which 3 were waited for; matrix products, arithmetic and copies ran while one was open for 1% of the time, Pallas kernels for 0%

profile of v1, /device:TPU:0, one launch (start us, length us, event | category | flops | bytes accessed | tf_op | source)
XLA Modules:
  0.0 495.8 jit_solution(6863971252179138947)
XLA Ops:
  7.2 0.0 copy-start
  7.2 0.0 all-reduce.4.cloned.1.call-start
  7.2 0.9 slice_multiply_fusion
  8.2 0.0 copy-start.1
  8.2 31.8 %fusion.11 = bf16[128,4096]{1,0:T(8,128)(2,1)S(1)} fusion(bf16[6,128,4096]{2,1,0:T(8,128)(2,1)} %param.6, f32[4096]{0:T(1024)S(1)} %bitcast.30, f32[4096]{0:T(1024)S(1)} %bitcast.29), kind=kLoop, calls=%fused_computation.30 | loop fusion | flops 36700160 | bytes 7372800 | tf_op jit(solution)/shard_map/convert_element_type | solution.py:46
  40.0 0.0 copy-done.1
  40.1 0.0 copy-start.2
  40.1 1.5 fusion.27
  41.6 0.0 copy-done.2
  41.6 2.0 convolution_bitcast_fusion
  43.6 0.0 all-reduce.4.cloned.1.call-update
  43.6 0.0 all-reduce.6.cloned.1.call-start
  43.7 0.0 copy-done
  43.7 1.1 fusion.26
  44.8 42.7 %all-reduce.4.cloned.1.call-done = f32[512,512]{0,1:T(8,128)} async-done(((f32[512,512]{0,1:T(8,128)}), f32[512,512]{0,1:T(8,128)}) %all-reduce.4.cloned.1.call-update) | async-done | bytes 1048592 | tf_op jit(solution)/shard_map/psum | solution.py:58
  87.5 0.0 all-reduce.6.cloned.1.call-update
  87.6 0.0 reduce-scatter.2.cloned.1.call-start
  87.6 3.5 fusion.23
  91.1 0.0 reduce-scatter.2.cloned.1.call-update
  91.1 350.5 %all-reduce.6.cloned.1.call-done = (f32[128,256]{1,0:T(8,128)}, f32[512,512]{0,1:T(8,128)}) async-done(((f32[128,256]{1,0:T(8,128)}, f32[512,512]{0,1:T(8,128)}), (f32[128,256]{1,0:T(8,128)}, f32[512,512]{0,1:T(8,128)})) %all-reduce.6.cloned.1.call-update) | async-done | bytes 1179664 | tf_op jit(solution)/shard_map/psum | solution.py:56
  441.7 0.0 copy-start.3
  441.7 2.6 copy.9
  444.2 44.4 %reduce-scatter.2.cloned.1.call-done = f32[64,4096]{1,0:T(8,128)} async-done(((f32[256,4096]{1,0:T(8,128)}), f32[64,4096]{1,0:T(8,128)}) %reduce-scatter.2.cloned.1.call-update) | async-done | bytes 1048592 | tf_op jit(solution)/shard_map/reduce_scatter | solution.py:63
  488.6 0.0 copy-done.3
  488.6 0.7 copy.13
Async XLA Ops:
  7.2 36.5 %copy-start = (bf16[4096,256]{1,0:T(8,128)(2,1)S(1)}, bf16[4096,256]{1,0:T(8,128)(2,1)}, u32[]{:S(2)}) copy-start(bf16[4096,256]{1,0:T(8,128)(2,1)} %param.8) | copy-start | bytes 6291460
  7.2 80.4 %all-reduce.4.cloned.1.call-start = ((), (), s32[]{:S(2)}) async-start(), calls=%async_computation.2 | async-start | bytes 2097152 | tf_op jit(solution)/shard_map/psum | solution.py:58
  8.2 31.9 %copy-start.1 = (bf16[512,4096]{1,0:T(8,128)(2,1)S(1)}, bf16[512,4096]{1,0:T(8,128)(2,1)}, u32[]{:S(2)}) copy-start(bf16[512,4096]{1,0:T(8,128)(2,1)} %param.11) | copy-start | bytes 12582916
  40.1 1.6 copy-start.2
  43.6 398.0 %all-reduce.6.cloned.1.call-start = ((), (), s32[]{:S(2)}) async-start(), calls=%async_computation.3 | async-start | bytes 2359296 | tf_op jit(solution)/shard_map/psum | solution.py:56
  87.6 401.1 %reduce-scatter.2.cloned.1.call-start = ((), (), s32[]{:S(2)}) async-start(), calls=%async_computation.1 | async-start | bytes 5242880 | tf_op jit(solution)/shard_map/reduce_scatter | solution.py:63
  441.7 47.0 %copy-start.3 = (f32[128,256]{1,0:T(8,128)S(1)}, f32[128,256]{1,0:T(8,128)}, u32[]{:S(2)}) copy-start(f32[128,256]{1,0:T(8,128)} %get-tuple-element.10) | copy-start | bytes 393220
Sparse Core Ops, SparseCore 0:
  43.8 43.7 all-reduce.3
  90.7 350.9 all-reduce.5
  444.6 43.9 reduce-scatter.1

commit v2 on v0

--- a/solution.py
+++ b/solution.py
@@ -3,6 +3,12 @@
 import jax.numpy as jnp
 from jax import lax
 from jax.sharding import PartitionSpec as P
+
+
+def gather_and_add(x, axis):
+    shards = lax.all_gather(x, axis, axis=0, tiled=False)
+    acc = shards.sum(axis=0)
+    return acc
 
 
 def energy_field(strains, moduli):
@@ -53,7 +59,7 @@
     cross_part = lax.dot_general(
         energy, core_right, (((1,), (1,)), ((), ())), preferred_element_type=jnp.float32
     )
-    range_sketch = lax.psum(range_part, "pts")
+    range_sketch = gather_and_add(range_part, "pts")
     core_share = jnp.dot(core_left, cross_part, precision=lax.Precision.HIGHEST)
     core_sketch = lax.psum(core_share, ("snap", "pts"))
     own_cols = lax.dynamic_slice_in_dim(

time: 557 us -> 266 us (0.48)
  waiting for transfers between devices: 496 us -> 202 us
    psum x1 -> x0, waiting for transfers between devices: 326 us -> none  [per_device(): range_sketch = lax.psum(range_part, 'pts')]
    reduce_scatter x1, waiting for transfers between devices: 0.01 us -> 42 us  [per_device(): lax.psum_scatter(jnp.dot(own_cols, energy, preferred_element_type=jnp.flo...]
    psum x1, waiting for transfers between devices: 171 us -> 160 us  [per_device(): core_sketch = lax.psum(core_share, ('snap', 'pts'))]
  transfers between devices with their start and end apart: 3 -> 3, of which waited for: 2 -> 2; matrix products, arithmetic and copies ran while one was open for 1% -> 4% of each run, Pallas kernels for 0% -> 0%
where the time goes in v2:
time: 266 us; the launch traced here: 264 us
  waiting for transfers between devices  202 us (76%)
  other arithmetic  35.9 us (13%)
  between operations  15.6 us (6%)
  matrix products  8.14 us (3%)
    psum x1, waiting for transfers between devices, per_device(): core_sketch = lax.psum(core_share, ('snap', 'pts'))  160 us
    reduce_scatter x1, waiting for transfers between devices, per_device(): lax.psum_scatter(jnp.dot(own_cols, energy, preferred_element_type=jnp.flo...  42 us
    convert_element_type x1, other arithmetic, energy_field(): return density.astype(jnp.bfloat16)  31.8 us
  transfers between devices with their start and end apart: 3, of which 2 were waited for; matrix products, arithmetic and copies ran while one was open for 4% of the time, Pallas kernels for 0%

profile of v2, /device:TPU:0, one launch (start us, length us, event | category | flops | bytes accessed | tf_op | source)
XLA Modules:
  0.0 264.3 jit_solution(1925088228369590594)
XLA Ops:
  8.0 0.0 copy-start
  8.0 0.0 all-reduce.2.cloned.1.call-start
  8.1 0.9 slice_multiply_fusion
  9.0 0.0 copy-start.1
  9.0 31.8 %fusion.11 = bf16[128,4096]{1,0:T(8,128)(2,1)S(1)} fusion(bf16[6,128,4096]{2,1,0:T(8,128)(2,1)} %param.6, f32[4096]{0:T(1024)S(1)} %bitcast.32, f32[4096]{0:T(1024)S(1)} %bitcast.31), kind=kLoop, calls=%fused_computation.30 | loop fusion | flops 36700160 | bytes 7372800 | tf_op jit(solution)/shard_map/convert_element_type | solution.py:52
  40.9 0.0 copy-done.1
  40.9 0.0 copy-start.2
  40.9 1.5 fusion.27
  42.4 0.0 copy-done.2
  42.4 2.0 convolution_bitcast_fusion
  44.4 0.0 all-reduce.2.cloned.1.call-update
  44.5 0.0 all-gather.3.cloned.1.call-start
  44.5 0.0 copy-done
  44.5 1.1 fusion.26
  45.6 0.0 all-gather.3.cloned.1.call-update
  45.7 0.0 reduce-scatter.2.cloned.1.call-start
  45.7 3.5 %fusion.23 = f32[256,4096]{1,0:T(8,128)} fusion(bf16[128,4096]{1,0:T(8,128)(2,1)S(1)} %fusion.11, bf16[256,512]{1,0:T(8,128)(2,1)} %param.9, s32[]{:T(128)S(6)} %select_n.3), kind=kOutput, calls=%fused_computation.43 | convolution fusion | flops 268435456 | bytes 5308420 | tf_op jit(solution)/shard_map/dot_general | solution.py:69
  49.2 0.0 reduce-scatter.2.cloned.1.call-update
  49.2 160.0 %all-reduce.2.cloned.1.call-done = f32[512,512]{0,1:T(8,128)} async-done(((f32[512,512]{0,1:T(8,128)}), f32[512,512]{0,1:T(8,128)}) %all-reduce.2.cloned.1.call-update) | async-done | bytes 1048592 | tf_op jit(solution)/shard_map/psum | solution.py:64
  209.3 2.5 copy.9
  211.8 0.0 all-gather.3.cloned.1.call-done
  211.8 3.1 %reduce_sum.9 = f32[128,256]{1,0:T(8,128)} reduce(f32[32,128,256]{2,1,0:T(8,128)} %bitcast.30, f32[]{:T(128)} %constant.8.clone.1), dimensions={0}, to_apply=%region_0.0 | reduce | flops 1015808 | bytes 4325380 | tf_op jit(solution)/shard_map/reduce_sum | solution.py:10
  214.9 42.0 %reduce-scatter.2.cloned.1.call-done = f32[64,4096]{1,0:T(8,128)} async-done(((f32[256,4096]{1,0:T(8,128)}), f32[64,4096]{1,0:T(8,128)}) %reduce-scatter.2.cloned.1.call-update) | async-done | bytes 1048592 | tf_op jit(solution)/shard_map/reduce_scatter | solution.py:68
Async XLA Ops:
  8.0 36.5 %copy-start = (bf16[4096,256]{1,0:T(8,128)(2,1)S(1)}, bf16[4096,256]{1,0:T(8,128)(2,1)}, u32[]{:S(2)}) copy-start(bf16[4096,256]{1,0:T(8,128)(2,1)} %param.8) | copy-start | bytes 6291460
  8.0 201.3 %all-reduce.2.cloned.1.call-start = ((), (), s32[]{:S(2)}) async-start(), calls=%async_computation.2 | async-start | bytes 2097152 | tf_op jit(solution)/shard_map/psum | solution.py:64
  9.0 31.9 %copy-start.1 = (bf16[512,4096]{1,0:T(8,128)(2,1)S(1)}, bf16[512,4096]{1,0:T(8,128)(2,1)}, u32[]{:S(2)}) copy-start(bf16[512,4096]{1,0:T(8,128)(2,1)} %param.11) | copy-start | bytes 12582916
  40.9 1.6 copy-start.2
  44.5 167.3 %all-gather.3.cloned.1.call-start = ((), (), s32[]{:S(2)}) async-start(), calls=%async_computation.3 | async-start | bytes 4325376 | tf_op jit(solution)/shard_map/all_gather | solution.py:9
  45.7 211.2 %reduce-scatter.2.cloned.1.call-start = ((), (), s32[]{:S(2)}) async-start(), calls=%async_computation.1 | async-start | bytes 5242880 | tf_op jit(solution)/shard_map/reduce_scatter | solution.py:68
Sparse Core Ops, SparseCore 0:
  44.6 164.6 all-reduce.1
  212.2 44.6 reduce-scatter.1
Sparse Core Ops, SparseCore 1:
  48.6 84.8 all-gather.2
